TPU v7x, 512 devices: a whole 4x8x8 slice. The times are simulated.
512 devices in a mesh: src: 8 (over z_lo, core), lat: 32 (over y, x), sub: 2 (over z_hi).
Axes of the slice: x: 4, y: 8, z: 8 (z_hi: 2, z_lo: 4; z = z_hi * 4 + z_lo), core: 2. Of those that a mesh axis runs over, the one named last changes fastest.
Arguments:
- sources: float32 [8, 24, 384, 8, 128], P(None, None, ('lat', 'sub'), 'src'), may hold values from -6 to 6
- eigvecs: bfloat16 [32, 24, 384, 8, 128], P(None, None, ('lat', 'sub'), 'src'), may hold values from -6 to 6
- eigvals: float32 [32], replicated, may hold values from 0.5 to 8
- links: float32 [4, 18, 384, 8, 128], P(None, None, ('lat', 'sub')), may hold values from -6 to 6
- damping: float32 [8], P('src'), may hold values from 0.5 to 1
Outputs:
- guess: float32 [8, 24, 384, 8, 128], P(None, None, ('lat', 'sub'), 'src')
- solution: float32 [8, 24, 384, 8, 128], P(None, None, ('lat', 'sub'), 'src')
All inputs are finite; a program needn't handle non-finite values.
Results may differ from a plain program's by a relative error of at most 0.0047.
Values sent between devices are 32-bit elements; how exact they have to be, the bound alone decides.
No kernel may reach another device: no remote copies, remote signals or barrier semaphores. Data moves between devices by JAX's collectives and lax.ppermute only.
A program may use at most 64 MiB of HBM per device.

v0:
```python
import math
import jax
import jax.numpy as jnp
import numpy as np
from jax import lax
from jax.sharding import PartitionSpec as P

LX = 16
ITERS = 2
HOPPING = 0.12
SPIN_BLOCKS = [
    (np.array([[0.0, 0.0], [0.0, 0.0]]), np.array([[0.0, 1.0], [1.0, 0.0]])),
    (np.array([[0.0, -1.0], [1.0, 0.0]]), np.zeros((2, 2))),
    (np.array([[0.0, 0.0], [0.0, 0.0]]), np.array([[1.0, 0.0], [0.0, -1.0]])),
    (np.eye(2), np.zeros((2, 2))),
]


def passed_along(x, axis, by):
    devices = lax.axis_size(axis)
    return lax.ppermute(x, axis, [(i, (i + by) % devices) for i in range(devices)])


def padded_2(x, sides, width):
    for axis, dim in sides:
        devices, length = (lax.axis_size(axis), x.shape[dim])
        up = [(i, (i + 1) % devices) for i in range(devices)]
        down = [(j, i) for i, j in up]
        last = lax.slice_in_dim(x, length - width, length, axis=dim)
        first = lax.slice_in_dim(x, 0, width, axis=dim)
        before = lax.ppermute(last, axis, up)
        after = lax.ppermute(first, axis, down)
        x = jnp.concatenate([before, x, after], axis=dim)
    return x


def spin_apply(table_re, table_im, real_part, imag_part):
    rows_re = []
    rows_im = []
    for row in range(2):
        acc_re = (
            float(table_re[row, 0]) * real_part[:, 0] - float(table_im[row, 0]) * imag_part[:, 0]
        )
        acc_im = (
            float(table_re[row, 0]) * imag_part[:, 0] + float(table_im[row, 0]) * real_part[:, 0]
        )
        acc_re = (
            acc_re
            + float(table_re[row, 1]) * real_part[:, 1]
            - float(table_im[row, 1]) * imag_part[:, 1]
        )
        acc_im = (
            acc_im
            + float(table_re[row, 1]) * imag_part[:, 1]
            + float(table_im[row, 1]) * real_part[:, 1]
        )
        rows_re.append(acc_re)
        rows_im.append(acc_im)
    return (jnp.stack(rows_re, 1), jnp.stack(rows_im, 1))


def project(sign, direction, real_part, imag_part):
    table_re, table_im = SPIN_BLOCKS[direction]
    lower_re, lower_im = spin_apply(table_re, table_im, real_part[:, 2:], imag_part[:, 2:])
    return (real_part[:, :2] + sign * lower_re, imag_part[:, :2] + sign * lower_im)


def rebuild(sign, direction, upper_re, upper_im):
    table_re, table_im = SPIN_BLOCKS[direction]
    lower_re, lower_im = spin_apply(table_re.T, -table_im.T, upper_re, upper_im)
    return (
        jnp.concatenate([upper_re, sign * lower_re], 1),
        jnp.concatenate([upper_im, sign * lower_im], 1),
    )


def color_mul(links_re, links_im, real_part, imag_part):
    rows_re = []
    rows_im = []
    for row in range(3):
        acc_re = links_re[row, 0] * real_part[:, :, 0] - links_im[row, 0] * imag_part[:, :, 0]
        acc_im = links_re[row, 0] * imag_part[:, :, 0] + links_im[row, 0] * real_part[:, :, 0]
        for col in range(1, 3):
            acc_re = (
                acc_re
                + links_re[row, col] * real_part[:, :, col]
                - links_im[row, col] * imag_part[:, :, col]
            )
            acc_im = (
                acc_im
                + links_re[row, col] * imag_part[:, :, col]
                + links_im[row, col] * real_part[:, :, col]
            )
        rows_re.append(acc_re)
        rows_im.append(acc_im)
    return (jnp.stack(rows_re, 2), jnp.stack(rows_im, 2))


def color_adj(links_re, links_im, real_part, imag_part):
    rows_re = []
    rows_im = []
    for row in range(3):
        acc_re = links_re[0, row] * real_part[:, :, 0] + links_im[0, row] * imag_part[:, :, 0]
        acc_im = links_re[0, row] * imag_part[:, :, 0] - links_im[0, row] * real_part[:, :, 0]
        for col in range(1, 3):
            acc_re = (
                acc_re
                + links_re[col, row] * real_part[:, :, col]
                + links_im[col, row] * imag_part[:, :, col]
            )
            acc_im = (
                acc_im
                + links_re[col, row] * imag_part[:, :, col]
                - links_im[col, row] * real_part[:, :, col]
            )
        rows_re.append(acc_re)
        rows_im.append(acc_im)
    return (jnp.stack(rows_re, 2), jnp.stack(rows_im, 2))


def link_parts(links, direction):
    extent = links.shape[2:]
    return (
        links[direction, :9].reshape((3, 3) + extent),
        links[direction, 9:].reshape((3, 3) + extent),
    )


def neighbour(values, direction, step):
    if direction == 0:
        column = jnp.arange(values.shape[-1]) % LX
        border = LX - 1 if step > 0 else 0
        inside = jnp.roll(values, -step, axis=-1)
        wrapped = jnp.roll(values, step * (LX - 1), axis=-1)
        return jnp.where(column == border, wrapped, inside)
    if direction == 1:
        return jnp.roll(values, -step * LX, axis=-1)
    return jnp.roll(values, -step, axis=-2)


def split_parts(spinor):
    count = spinor.shape[0]
    extent = spinor.shape[2:]
    return (
        spinor[:, :12].reshape((count, 4, 3) + extent),
        spinor[:, 12:].reshape((count, 4, 3) + extent),
    )


def join_parts(real_part, imag_part):
    count = real_part.shape[0]
    extent = real_part.shape[3:]
    return jnp.concatenate(
        [real_part.reshape((count, 12) + extent), imag_part.reshape((count, 12) + extent)], 1
    )


def shards(sources, eigvecs, eigvals, links, damping):
    count = sources.shape[0]
    flat_src = sources.astype(jnp.bfloat16).reshape(count, 24, -1)
    swapped = jnp.concatenate([flat_src[:, 12:], -flat_src[:, :12]], 1)
    stacked = jnp.concatenate([flat_src, swapped], 0).reshape(2 * count, -1)
    flat_vec = eigvecs.reshape(eigvecs.shape[0], -1)
    partial_value = lax.dot_general(
        flat_vec, stacked, (((1,), (1,)), ((), ())), preferred_element_type=jnp.float32
    )
    correlation = lax.psum(partial_value, ("src", "lat", "sub"))
    sites_all = flat_vec.shape[1] // 24 * lax.axis_size(("src", "lat", "sub"))
    correlation = correlation / math.sqrt(24 * sites_all)
    weights = (
        jnp.concatenate([correlation[:, :count].T, correlation[:, count:].T], 0) / eigvals[None, :]
    )
    weights = weights.astype(jnp.bfloat16)
    mixed = jnp.dot(weights, flat_vec, preferred_element_type=jnp.float32)
    middle = mixed.shape[1] // 2
    guess = jnp.concatenate(
        [
            mixed[:count, :middle] - mixed[count:, middle:],
            mixed[:count, middle:] + mixed[count:, :middle],
        ],
        1,
    ).reshape(sources.shape)
    source, iterate = (
        lax.all_to_all(sources, "src", split_axis=0, concat_axis=3, tiled=True),
        lax.all_to_all(guess, "src", split_axis=0, concat_axis=3, tiled=True),
    )
    extent = lax.axis_size(("lat", "sub"))
    place = lax.axis_index(("lat", "sub"))
    slices = links.shape[2]
    slice_index = jnp.arange(slices)
    top_flip = jnp.where(place == extent - 1, -1.0, 1.0)
    bottom_flip = jnp.where(place == 0, -1.0, 1.0)
    top_sign = jnp.where(slice_index == slices - 1, top_flip, 1.0).astype(jnp.float32)[
        :, None, None
    ]
    bottom_sign = jnp.where(slice_index == 0, bottom_flip, 1.0).astype(jnp.float32)[:, None, None]
    time_re, time_im = link_parts(links, 3)
    space_links = []
    for direction in range(3):
        links_re, links_im = link_parts(links, direction)
        space_links.append(
            (
                links_re,
                links_im,
                neighbour(links_re, direction, -1),
                neighbour(links_im, direction, -1),
            )
        )
    rim_links = passed_along(links[3, :, slices - 1 :], ("lat", "sub"), 1)
    behind_links = jnp.concatenate([rim_links, links[3, :, : slices - 1]], 1)
    back_re = behind_links[:9].reshape((3, 3) + behind_links.shape[1:])
    back_im = behind_links[9:].reshape((3, 3) + behind_links.shape[1:])
    rate = damping[:, None, None, None, None]
    for sweep in range(ITERS):
        real_part, imag_part = split_parts(iterate)
        terms = []
        for apply_direction in range(3):
            apply_links_re, apply_links_im, behind_lre, behind_lim = space_links[apply_direction]
            ahead_re = neighbour(real_part, apply_direction, 1)
            ahead_im = neighbour(imag_part, apply_direction, 1)
            carried = color_mul(apply_links_re, apply_links_im, ahead_re, ahead_im)
            terms.append(rebuild(-1.0, apply_direction, *project(-1.0, apply_direction, *carried)))
            behind_re = neighbour(real_part, apply_direction, -1)
            behind_im = neighbour(imag_part, apply_direction, -1)
            carried = color_adj(behind_lre, behind_lim, behind_re, behind_im)
            terms.append(rebuild(1.0, apply_direction, *project(1.0, apply_direction, *carried)))
        padded = padded_2(iterate, ((("lat", "sub"), 2),), 1)
        ahead_re, ahead_im = split_parts(padded[:, :, 2:] * top_sign)
        carried = color_mul(time_re, time_im, ahead_re, ahead_im)
        terms.append(rebuild(-1.0, 3, *project(-1.0, 3, *carried)))
        behind_re, behind_im = split_parts(padded[:, :, :slices] * bottom_sign)
        carried = color_adj(back_re, back_im, behind_re, behind_im)
        terms.append(rebuild(1.0, 3, *project(1.0, 3, *carried)))
        total_re, total_im = terms[0]
        for extra in terms[1:]:
            total_re = total_re + extra[0]
            total_im = total_im + extra[1]
        iterate = iterate + rate * (source - (iterate - HOPPING * join_parts(total_re, total_im)))
    solution = lax.all_to_all(iterate, "src", split_axis=3, concat_axis=0, tiled=True)
    return (guess, solution)


def solution(mesh):
    return jax.shard_map(
        shards,
        mesh=mesh,
        in_specs=(
            P(None, None, ("lat", "sub"), "src", None),
            P(None, None, ("lat", "sub"), "src", None),
            P(),
            P(None, None, ("lat", "sub"), None, None),
            P("src"),
        ),
        out_specs=(
            P(None, None, ("lat", "sub"), "src", None),
            P(None, None, ("lat", "sub"), "src", None),
        ),
        check_vma=False,
    )
```

profile of v0, /device:TPU:1, one launch (start us, length us, event | category | flops | bytes accessed | tf_op | source)
XLA Modules:
  0.0 232.8 jit_solution(8140742136384353029)
XLA Ops:
  0.6 2.6 %convert_reduce_fusion = bf16[8,24,6,128]{3,2,1,0:T(8,128)(2,1)S(1)} fusion(f32[8,24,6,1,128]{4,3,2,1,0:T(1,128)} %param.5), kind=kLoop, calls=%fused_computation.40 | loop fusion | flops 147456 | bytes 884736 | tf_op jit(solution)/shard_map/convert_element_type | solution.py:160
  3.6 1.0 concatenate.768
  4.7 1.6 copy.464
  6.3 1.3 reshape.6010
  9.0 106.1 %psum.7 = f32[32,16]{0,1:T(8,128)S(1)} all-reduce(f32[32,16]{0,1:T(8,128)S(1)} %convolution_bitcast_fusion), channel_id=1, replica_groups=mesh['src'=8,'lat'=32,'sub'=2] {'src','lat','sub'}, use_global_device_ids=true, to_apply=%region_0.0 | all-reduce | flops 512 | bytes 4096 | tf_op jit(solution)/shard_map/psum | solution.py:167
  115.6 1.0 copy.465
  116.6 4.1 %all-to-all-start = ((f32[8,24,6,1,128]{4,1,3,2,0:T(8,128)}), f32[8,24,6,1,128]{4,1,3,2,0:T(8,128)S(1)}, u32[]{:S(2)}, u32[]{:S(2)}) async-start(f32[8,24,6,1,128]{4,1,3,2,0:T(8,128)} %copy.465), calls=%async_computation | async-start | bytes 1179648 | tf_op jit(solution)/shard_map/all_to_all | solution.py:185
  120.7 0.9 slice_bitcast_fusion.1
  121.6 4.1 %collective-permute-start.1 = (f32[18,1,8,128]{3,2,1,0:T(8,128)S(1)}, f32[18,1,8,128]{3,2,1,0:T(8,128)}, u32[]{:S(2)}, u32[]{:S(2)}) collective-permute-start(f32[18,1,8,128]{3,2,1,0:T(8,128)S(1)} %slice_bitcast_fusion.1), channel_id=1, source_target_pairs={{0,1},{1,2},{2,3},{3,4},{4,5},{5,6},{6,7},{7,8},{8,9},{9,10},{10,1... | collective-permute-start | bytes 221192 | tf_op jit(solution)/shard_map/ppermute | solution.py:21
  125.7 2.4 %fusion.194 = (f32[1,9,6,8,128]{4,3,2,1,0:T(8,128)S(1)}, f32[1,9,6,8,128]{4,3,2,1,0:T(8,128)}, f32[1,9,6,8,128]{4,3,2,1,0:T(8,128)S(1)}, f32[1,9,6,8,128]{4,3,2,...) fusion(f32[4,18,6,8,128]{4,3,2,1,0:T(8,128)} %param.8), kind=kLoop, calls=%fused_computation.843 | loop fusion | bytes 3538944 | tf_op jit(solution)/shard_map/slice | solution.py:124
  128.1 0.8 slice.1779
  128.9 0.8 slice.1781
  129.7 0.8 slice_bitcast_fusion.108
  130.5 0.8 slice.1791
  131.3 0.8 slice.1789
  132.1 0.8 slice.3635
  133.7 0.8 slice.3627
  134.6 0.8 slice_bitcast_fusion.48
  135.4 0.9 copy.467
  136.9 1.6 maximum_select_fusion.8
  143.0 1.0 slice_bitcast_fusion
  144.1 0.8 fusion.39
  145.8 5.4 %all-to-all-start.1 = ((f32[8,24,6,1,128]{4,1,3,2,0:T(8,128)}), f32[8,24,6,1,128]{4,1,3,2,0:T(8,128)S(1)}, u32[]{:S(2)}, u32[]{:S(2)}) async-start(f32[8,24,6,1,128]{4,1,3,2,0:T(8,128)} %copy.467), calls=%async_computation.1 | async-start | bytes 1179648 | tf_op jit(solution)/shard_map/all_to_all | solution.py:184
  153.3 5.4 %collective-permute-start.2 = (f32[1,24,1,8,128]{4,3,2,1,0:T(8,128)S(1)}, f32[1,24,1,8,128]{4,3,2,1,0:T(8,128)S(1)}, u32[]{:S(2)}, u32[]{:S(2)}) collective-permute-start(f32[1,24,1,8,128]{4,3,2,1,0:T(8,128)S(1)} %get-tuple-element.256), channel_id=1, source_target_pairs={{0,1},{1,2},{2,3},{3,4},{4,5},{5,6},{6,7},{7,8},{8,9},{9,10},{10,1... | collective-permute-start | bytes 294920 | tf_op jit(solution)/shard_map/ppermute | solution.py:31
  158.7 8.2 %collective-permute-start = (f32[1,24,1,8,128]{4,3,2,1,0:T(8,128)S(1)}, f32[1,24,1,8,128]{4,3,2,1,0:T(8,128)S(1)}, u32[]{:S(2)}, u32[]{:S(2)}) collective-permute-start(f32[1,24,1,8,128]{4,3,2,1,0:T(8,128)S(1)} %get-tuple-element.257), channel_id=1, source_target_pairs={{1,0},{2,1},{3,2},{4,3},{5,4},{6,5},{7,6},{8,7},{9,8},{10,9},{11,1... | collective-permute-start | bytes 294920 | tf_op jit(solution)/shard_map/ppermute | solution.py:32
  189.2 1.9 collective-permute-start.4
  191.2 11.5 %collective-permute-start.3 = (f32[1,24,1,8,128]{4,3,2,1,0:T(8,128)S(1)}, f32[1,24,1,8,128]{4,3,2,1,0:T(8,128)S(1)}, u32[]{:S(2)}, u32[]{:S(2)}) collective-permute-start(f32[1,24,1,8,128]{4,3,2,1,0:T(8,128)S(1)} %get-tuple-element.243), channel_id=1, source_target_pairs={{1,0},{2,1},{3,2},{4,3},{5,4},{6,5},{7,6},{8,7},{9,8},{10,9},{11,1... | collective-permute-start | bytes 294920 | tf_op jit(solution)/shard_map/ppermute | solution.py:32
  207.8 1.0 copy.470
  208.8 6.8 %all-to-all-start.2 = ((f32[1,24,6,8,128]{4,1,2,0,3:T(8,128)}), f32[1,24,6,8,128]{4,1,2,0,3:T(8,128)S(1)}, u32[]{:S(2)}, u32[]{:S(2)}) async-start(f32[1,24,6,8,128]{4,1,2,0,3:T(8,128)} %copy.470), calls=%async_computation.2 | async-start | bytes 1179648 | tf_op jit(solution)/shard_map/all_to_all | solution.py:239
  215.6 1.4 copy.472
  217.0 14.3 %all-to-all-done.2 = f32[1,24,6,8,128]{4,1,2,0,3:T(8,128)S(1)} async-done(((f32[1,24,6,8,128]{4,1,2,0,3:T(8,128)}), f32[1,24,6,8,128]{4,1,2,0,3:T(8,128)S(1)}, u32[]{:S(2)}, u32[]{:S(2)}) %all-to-all-start.2) | async-done | bytes 589856 | tf_op jit(solution)/shard_map/all_to_all | solution.py:239
  231.3 1.4 copy.473
  (748 shorter events, 34.0 us)
Async XLA Ops:
  7.7 1.0 copy-start.13
  7.8 107.3 %copy-start.254 = (f32[32]{0:T(128)S(1)}, f32[32]{0:T(128)}, u32[]{:S(2)}) copy-start(f32[32]{0:T(128)} %param.7) | copy-start | bytes 388
  116.6 29.2 %all-to-all-start = ((f32[8,24,6,1,128]{4,1,3,2,0:T(8,128)}), f32[8,24,6,1,128]{4,1,3,2,0:T(8,128)S(1)}, u32[]{:S(2)}, u32[]{:S(2)}) async-start(f32[8,24,6,1,128]{4,1,3,2,0:T(8,128)} %copy.465), calls=%async_computation | async-start | bytes 1179648 | tf_op jit(solution)/shard_map/all_to_all | solution.py:185
  121.6 22.5 %collective-permute-start.1 = (f32[18,1,8,128]{3,2,1,0:T(8,128)S(1)}, f32[18,1,8,128]{3,2,1,0:T(8,128)}, u32[]{:S(2)}, u32[]{:S(2)}) collective-permute-start(f32[18,1,8,128]{3,2,1,0:T(8,128)S(1)} %slice_bitcast_fusion.1), channel_id=1, source_target_pairs={{0,1},{1,2},{2,3},{3,4},{4,5},{5,6},{6,7},{7,8},{8,9},{9,10},{10,1... | collective-permute-start | bytes 221192 | tf_op jit(solution)/shard_map/ppermute | solution.py:21
  132.9 2.5 %copy-start = (f32[8,24,6,1,128]{4,3,2,1,0:T(1,128)S(1)}, f32[8,24,6,1,128]{4,3,2,1,0:T(1,128)}, u32[]{:S(2)}) copy-start(f32[8,24,6,1,128]{4,3,2,1,0:T(1,128)} %param.5) | copy-start | bytes 1769476
  136.9 2.4 %copy-start.2 = (f32[3,3,6,8,16]{4,3,2,1,0:T(8,128)S(1)}, f32[3,3,6,8,16]{4,3,2,1,0:T(8,128)}, u32[]{:S(2)}) copy-start(f32[3,3,6,8,16]{4,3,2,1,0:T(8,128)} %slice.3635) | copy-start | bytes 82948
  138.5 1.6 copy-start.3
  139.3 30.4 %copy-start.170 = (f32[6,8,128]{2,1,0:T(8,128)}, f32[6,8,128]{2,1,0:T(8,128)S(1)}, u32[]{:S(2)}) copy-start(f32[6,8,128]{2,1,0:T(8,128)S(1)} %get-tuple-element.563) | copy-start | bytes 73732
  139.3 30.4 %copy-start.172 = (f32[6,8,128]{2,1,0:T(8,128)}, f32[6,8,128]{2,1,0:T(8,128)S(1)}, u32[]{:S(2)}) copy-start(f32[6,8,128]{2,1,0:T(8,128)S(1)} %get-tuple-element.570) | copy-start | bytes 73732
  139.3 30.4 %copy-start.174 = (f32[6,8,128]{2,1,0:T(8,128)}, f32[6,8,128]{2,1,0:T(8,128)S(1)}, u32[]{:S(2)}) copy-start(f32[6,8,128]{2,1,0:T(8,128)S(1)} %get-tuple-element.571) | copy-start | bytes 73732
  139.3 30.5 %copy-start.176 = (f32[6,8,128]{2,1,0:T(8,128)}, f32[6,8,128]{2,1,0:T(8,128)S(1)}, u32[]{:S(2)}) copy-start(f32[6,8,128]{2,1,0:T(8,128)S(1)} %get-tuple-element.613) | copy-start | bytes 73732
  139.3 30.5 %copy-start.178 = (f32[6,8,128]{2,1,0:T(8,128)}, f32[6,8,128]{2,1,0:T(8,128)S(1)}, u32[]{:S(2)}) copy-start(f32[6,8,128]{2,1,0:T(8,128)S(1)} %get-tuple-element.614) | copy-start | bytes 73732
  139.3 30.5 %copy-start.180 = (f32[6,8,128]{2,1,0:T(8,128)}, f32[6,8,128]{2,1,0:T(8,128)S(1)}, u32[]{:S(2)}) copy-start(f32[6,8,128]{2,1,0:T(8,128)S(1)} %get-tuple-element.621) | copy-start | bytes 73732
  139.3 3.0 %copy-start.1 = (f32[1,9,6,8,128]{4,3,2,1,0:T(8,128)S(1)}, f32[1,9,6,8,128]{4,3,2,1,0:T(8,128)}, u32[]{:S(2)}) copy-start(f32[1,9,6,8,128]{4,3,2,1,0:T(8,128)} %get-tuple-element.149) | copy-start | bytes 663556
  143.0 34.6 %copy-start.26 = (f32[6,8,128]{2,1,0:T(8,128)}, f32[6,8,128]{2,1,0:T(8,128)S(1)}, u32[]{:S(2)}) copy-start(f32[6,8,128]{2,1,0:T(8,128)S(1)} %get-tuple-element.509) | copy-start | bytes 73732
  143.0 34.6 %copy-start.28 = (f32[6,8,128]{2,1,0:T(8,128)}, f32[6,8,128]{2,1,0:T(8,128)S(1)}, u32[]{:S(2)}) copy-start(f32[6,8,128]{2,1,0:T(8,128)S(1)} %get-tuple-element.516) | copy-start | bytes 73732
  143.0 34.6 %copy-start.30 = (f32[6,8,128]{2,1,0:T(8,128)}, f32[6,8,128]{2,1,0:T(8,128)S(1)}, u32[]{:S(2)}) copy-start(f32[6,8,128]{2,1,0:T(8,128)S(1)} %get-tuple-element.517) | copy-start | bytes 73732
  143.0 34.6 %copy-start.32 = (f32[6,8,128]{2,1,0:T(8,128)}, f32[6,8,128]{2,1,0:T(8,128)S(1)}, u32[]{:S(2)}) copy-start(f32[6,8,128]{2,1,0:T(8,128)S(1)} %get-tuple-element.650) | copy-start | bytes 73732
  143.0 34.6 %copy-start.34 = (f32[6,8,128]{2,1,0:T(8,128)}, f32[6,8,128]{2,1,0:T(8,128)S(1)}, u32[]{:S(2)}) copy-start(f32[6,8,128]{2,1,0:T(8,128)S(1)} %get-tuple-element.651) | copy-start | bytes 73732
  143.0 34.6 %copy-start.36 = (f32[6,8,128]{2,1,0:T(8,128)}, f32[6,8,128]{2,1,0:T(8,128)S(1)}, u32[]{:S(2)}) copy-start(f32[6,8,128]{2,1,0:T(8,128)S(1)} %get-tuple-element.658) | copy-start | bytes 73732
  145.7 33.2 %copy-start.14 = (f32[6,8,128]{2,1,0:T(8,128)}, f32[6,8,128]{2,1,0:T(8,128)S(1)}, u32[]{:S(2)}) copy-start(f32[6,8,128]{2,1,0:T(8,128)S(1)} %get-tuple-element.491) | copy-start | bytes 73732
  145.7 33.2 %copy-start.16 = (f32[6,8,128]{2,1,0:T(8,128)}, f32[6,8,128]{2,1,0:T(8,128)S(1)}, u32[]{:S(2)}) copy-start(f32[6,8,128]{2,1,0:T(8,128)S(1)} %get-tuple-element.498) | copy-start | bytes 73732
  145.7 33.2 %copy-start.18 = (f32[6,8,128]{2,1,0:T(8,128)}, f32[6,8,128]{2,1,0:T(8,128)S(1)}, u32[]{:S(2)}) copy-start(f32[6,8,128]{2,1,0:T(8,128)S(1)} %get-tuple-element.499) | copy-start | bytes 73732
  145.7 33.2 %copy-start.20 = (f32[6,8,128]{2,1,0:T(8,128)}, f32[6,8,128]{2,1,0:T(8,128)S(1)}, u32[]{:S(2)}) copy-start(f32[6,8,128]{2,1,0:T(8,128)S(1)} %get-tuple-element.659) | copy-start | bytes 73732
  145.7 33.2 %copy-start.22 = (f32[6,8,128]{2,1,0:T(8,128)}, f32[6,8,128]{2,1,0:T(8,128)S(1)}, u32[]{:S(2)}) copy-start(f32[6,8,128]{2,1,0:T(8,128)S(1)} %get-tuple-element.660) | copy-start | bytes 73732
  145.7 33.2 %copy-start.24 = (f32[6,8,128]{2,1,0:T(8,128)}, f32[6,8,128]{2,1,0:T(8,128)S(1)}, u32[]{:S(2)}) copy-start(f32[6,8,128]{2,1,0:T(8,128)S(1)} %get-tuple-element.667) | copy-start | bytes 73732
  145.8 33.9 %all-to-all-start.1 = ((f32[8,24,6,1,128]{4,1,3,2,0:T(8,128)}), f32[8,24,6,1,128]{4,1,3,2,0:T(8,128)S(1)}, u32[]{:S(2)}, u32[]{:S(2)}) async-start(f32[8,24,6,1,128]{4,1,3,2,0:T(8,128)} %copy.467), calls=%async_computation.1 | async-start | bytes 1179648 | tf_op jit(solution)/shard_map/all_to_all | solution.py:184
  153.3 23.1 %collective-permute-start.2 = (f32[1,24,1,8,128]{4,3,2,1,0:T(8,128)S(1)}, f32[1,24,1,8,128]{4,3,2,1,0:T(8,128)S(1)}, u32[]{:S(2)}, u32[]{:S(2)}) collective-permute-start(f32[1,24,1,8,128]{4,3,2,1,0:T(8,128)S(1)} %get-tuple-element.256), channel_id=1, source_target_pairs={{0,1},{1,2},{2,3},{3,4},{4,5},{5,6},{6,7},{7,8},{8,9},{9,10},{10,1... | collective-permute-start | bytes 294920 | tf_op jit(solution)/shard_map/ppermute | solution.py:31
  158.7 17.8 %collective-permute-start = (f32[1,24,1,8,128]{4,3,2,1,0:T(8,128)S(1)}, f32[1,24,1,8,128]{4,3,2,1,0:T(8,128)S(1)}, u32[]{:S(2)}, u32[]{:S(2)}) collective-permute-start(f32[1,24,1,8,128]{4,3,2,1,0:T(8,128)S(1)} %get-tuple-element.257), channel_id=1, source_target_pairs={{1,0},{2,1},{3,2},{4,3},{5,4},{6,5},{7,6},{8,7},{9,8},{10,9},{11,1... | collective-permute-start | bytes 294920 | tf_op jit(solution)/shard_map/ppermute | solution.py:32
  189.2 15.0 %collective-permute-start.4 = (f32[1,24,1,8,128]{4,3,2,1,0:T(8,128)S(1)}, f32[1,24,1,8,128]{4,3,2,1,0:T(8,128)S(1)}, u32[]{:S(2)}, u32[]{:S(2)}) collective-permute-start(f32[1,24,1,8,128]{4,3,2,1,0:T(8,128)S(1)} %get-tuple-element.242), channel_id=1, source_target_pairs={{0,1},{1,2},{2,3},{3,4},{4,5},{5,6},{6,7},{7,8},{8,9},{9,10},{10,1... | collective-permute-start | bytes 294920 | tf_op jit(solution)/shard_map/ppermute | solution.py:31
  191.2 13.1 %collective-permute-start.3 = (f32[1,24,1,8,128]{4,3,2,1,0:T(8,128)S(1)}, f32[1,24,1,8,128]{4,3,2,1,0:T(8,128)S(1)}, u32[]{:S(2)}, u32[]{:S(2)}) collective-permute-start(f32[1,24,1,8,128]{4,3,2,1,0:T(8,128)S(1)} %get-tuple-element.243), channel_id=1, source_target_pairs={{1,0},{2,1},{3,2},{4,3},{5,4},{6,5},{7,6},{8,7},{9,8},{10,9},{11,1... | collective-permute-start | bytes 294920 | tf_op jit(solution)/shard_map/ppermute | solution.py:32
  208.8 22.5 %all-to-all-start.2 = ((f32[1,24,6,8,128]{4,1,2,0,3:T(8,128)}), f32[1,24,6,8,128]{4,1,2,0,3:T(8,128)S(1)}, u32[]{:S(2)}, u32[]{:S(2)}) async-start(f32[1,24,6,8,128]{4,1,2,0,3:T(8,128)} %copy.470), calls=%async_computation.2 | async-start | bytes 1179648 | tf_op jit(solution)/shard_map/all_to_all | solution.py:239
  (231 other events, 183.7 us)
where the time goes:
time: 235 us; the launch traced here: 233 us
  blocking collectives  106 us (45%)
  starting transfers between devices  47.4 us (20%)
  local copies, waits for them, and re-layouts  38.7 us (16%)
  other arithmetic  20.1 us (9%)
  waiting for transfers between devices  14.4 us (6%)
  between operations  5.37 us (2%)
    psum x1, blocking collectives, shards(): correlation = lax.psum(partial_value, ('src', 'lat', 'sub'))  106 us
    ppermute x2, starting transfers between devices, padded_2(): after = lax.ppermute(first, axis, down)  19.7 us
    unnamed x515, local copies, waits for them, and re-layouts  15.9 us
    all_to_all x1, waiting for transfers between devices, shards(): lax.all_to_all(iterate, 'src', split_axis=3, concat_axis=0, tiled=True)  14.3 us
    ppermute x2, starting transfers between devices, padded_2(): before = lax.ppermute(last, axis, up)  7.3 us
    all_to_all x1, starting transfers between devices, shards(): lax.all_to_all(iterate, 'src', split_axis=3, concat_axis=0, tiled=True)  6.78 us
    all_to_all x1, starting transfers between devices, shards(): lax.all_to_all(sources, 'src', split_axis=0, concat_axis=3, tiled=True)  5.39 us
  transfers between devices with their start and end apart: 8, of which 1 were waited for; matrix products, arithmetic and copies ran while one was open for 13% of the time, Pallas kernels for 0%

commit v1 on v0

--- a/solution.py
+++ b/solution.py
@@ -164,7 +164,7 @@
     partial_value = lax.dot_general(
         flat_vec, stacked, (((1,), (1,)), ((), ())), preferred_element_type=jnp.float32
     )
-    correlation = lax.psum(partial_value, ("src", "lat", "sub"))
+    correlation = lax.psum(lax.psum(partial_value, "src"), ("lat", "sub"))
     sites_all = flat_vec.shape[1] // 24 * lax.axis_size(("src", "lat", "sub"))
     correlation = correlation / math.sqrt(24 * sites_all)
     weights = (

time: 235 us -> 375 us (1.60)
  blocking collectives: 106 us -> 218 us
  starting transfers between devices: 47.4 us -> 75.6 us
    psum x1 -> x2, blocking collectives: 106 us -> 218 us  [shards(): correlation = lax.psum(lax.psum(partial_value, 'src'), ('lat', 'sub'))]
    all_to_all x1, starting transfers between devices: 4.11 us -> 34.7 us  [shards(): lax.all_to_all(guess, 'src', split_axis=0, concat_axis=3, tiled=True)]
  transfers between devices with their start and end apart: 8 -> 8, of which waited for: 1 -> 1; matrix products, arithmetic and copies ran while one was open for 13% -> 8% of each run, Pallas kernels for 0% -> 0%
where the time goes in v1:
time: 375 us; the launch traced here: 373 us
  blocking collectives  218 us (58%)
  starting transfers between devices  75.6 us (20%)
  local copies, waits for them, and re-layouts  38.8 us (10%)
  other arithmetic  20.2 us (5%)
  waiting for transfers between devices  14.4 us (4%)
  between operations  5.4 us (1%)
    psum x2, blocking collectives, shards(): correlation = lax.psum(lax.psum(partial_value, 'src'), ('lat', 'sub'))  218 us
    all_to_all x1, starting transfers between devices, shards(): lax.all_to_all(guess, 'src', split_axis=0, concat_axis=3, tiled=True)  34.7 us
    ppermute x2, starting transfers between devices, padded_2(): after = lax.ppermute(first, axis, down)  21.3 us
    unnamed x515, local copies, waits for them, and re-layouts  15.9 us
    all_to_all x1, waiting for transfers between devices, shards(): lax.all_to_all(iterate, 'src', split_axis=3, concat_axis=0, tiled=True)  14.3 us
  transfers between devices with their start and end apart: 8, of which 1 were waited for; matrix products, arithmetic and copies ran while one was open for 8% of the time, Pallas kernels for 0%

profile of v1, /device:TPU:1, one launch (start us, length us, event | category | flops | bytes accessed | tf_op | source)
XLA Modules:
  0.0 373.0 jit_solution(18305963127304085714)
XLA Ops:
  0.6 2.6 convert_reduce_fusion
  3.6 1.0 concatenate.768
  4.7 1.6 copy.464
  6.3 1.3 reshape.6010
  9.0 20.0 %psum.14 = f32[32,16]{0,1:T(8,128)S(1)} all-reduce(f32[32,16]{0,1:T(8,128)S(1)} %convolution_bitcast_fusion), channel_id=1, replica_groups=mesh['src'=8,'lat'=32,'sub'=2] {'src'}, use_global_device_ids=true, to_apply=%region_0.0 | all-reduce | flops 512 | bytes 4096 | tf_op jit(solution)/shard_map/psum | solution.py:167
  29.0 198.1 %psum.15 = f32[32,16]{0,1:T(8,128)S(1)} all-reduce(f32[32,16]{0,1:T(8,128)S(1)} %psum.14), channel_id=1, replica_groups=mesh['src'=8,'lat'=32,'sub'=2] {'lat','sub'}, use_global_device_ids=true, to_apply=%region_1.0 | all-reduce | flops 512 | bytes 4096 | tf_op jit(solution)/shard_map/psum | solution.py:167
  227.6 1.0 copy.465
  228.6 34.7 %all-to-all-start = ((f32[8,24,6,1,128]{4,1,3,2,0:T(8,128)}), f32[8,24,6,1,128]{4,1,3,2,0:T(8,128)S(1)}, u32[]{:S(2)}, u32[]{:S(2)}) async-start(f32[8,24,6,1,128]{4,1,3,2,0:T(8,128)} %copy.465), calls=%async_computation | async-start | bytes 1179648 | tf_op jit(solution)/shard_map/all_to_all | solution.py:185
  263.3 0.9 slice_bitcast_fusion.1
  264.2 1.9 collective-permute-start.1
  266.2 2.4 fusion.194
  268.5 0.8 slice.1779
  269.4 0.8 slice.1781
  271.0 0.8 slice.1791
  271.8 0.8 slice.1789
  272.6 0.8 slice.3635
  274.2 0.8 slice.3627
  275.1 0.8 slice_bitcast_fusion.48
  275.9 0.9 copy.467
  277.4 1.6 maximum_select_fusion.8
  283.6 1.0 slice_bitcast_fusion
  284.7 0.8 fusion.39
  286.3 5.1 %all-to-all-start.1 = ((f32[8,24,6,1,128]{4,1,3,2,0:T(8,128)}), f32[8,24,6,1,128]{4,1,3,2,0:T(8,128)S(1)}, u32[]{:S(2)}, u32[]{:S(2)}) async-start(f32[8,24,6,1,128]{4,1,3,2,0:T(8,128)} %copy.467), calls=%async_computation.1 | async-start | bytes 1179648 | tf_op jit(solution)/shard_map/all_to_all | solution.py:184
  293.6 4.1 %collective-permute-start.2 = (f32[1,24,1,8,128]{4,3,2,1,0:T(8,128)S(1)}, f32[1,24,1,8,128]{4,3,2,1,0:T(8,128)S(1)}, u32[]{:S(2)}, u32[]{:S(2)}) collective-permute-start(f32[1,24,1,8,128]{4,3,2,1,0:T(8,128)S(1)} %get-tuple-element.256), channel_id=1, source_target_pairs={{0,1},{1,2},{2,3},{3,4},{4,5},{5,6},{6,7},{7,8},{8,9},{9,10},{10,1... | collective-permute-start | bytes 294920 | tf_op jit(solution)/shard_map/ppermute | solution.py:31
  297.6 9.8 %collective-permute-start = (f32[1,24,1,8,128]{4,3,2,1,0:T(8,128)S(1)}, f32[1,24,1,8,128]{4,3,2,1,0:T(8,128)S(1)}, u32[]{:S(2)}, u32[]{:S(2)}) collective-permute-start(f32[1,24,1,8,128]{4,3,2,1,0:T(8,128)S(1)} %get-tuple-element.257), channel_id=1, source_target_pairs={{1,0},{2,1},{3,2},{4,3},{5,4},{6,5},{7,6},{8,7},{9,8},{10,9},{11,1... | collective-permute-start | bytes 294920 | tf_op jit(solution)/shard_map/ppermute | solution.py:32
  329.8 1.9 collective-permute-start.4
  331.7 11.5 %collective-permute-start.3 = (f32[1,24,1,8,128]{4,3,2,1,0:T(8,128)S(1)}, f32[1,24,1,8,128]{4,3,2,1,0:T(8,128)S(1)}, u32[]{:S(2)}, u32[]{:S(2)}) collective-permute-start(f32[1,24,1,8,128]{4,3,2,1,0:T(8,128)S(1)} %get-tuple-element.243), channel_id=1, source_target_pairs={{1,0},{2,1},{3,2},{4,3},{5,4},{6,5},{7,6},{8,7},{9,8},{10,9},{11,1... | collective-permute-start | bytes 294920 | tf_op jit(solution)/shard_map/ppermute | solution.py:32
  348.4 1.0 copy.470
  349.4 6.5 %all-to-all-start.2 = ((f32[1,24,6,8,128]{4,1,2,0,3:T(8,128)}), f32[1,24,6,8,128]{4,1,2,0,3:T(8,128)S(1)}, u32[]{:S(2)}, u32[]{:S(2)}) async-start(f32[1,24,6,8,128]{4,1,2,0,3:T(8,128)} %copy.470), calls=%async_computation.2 | async-start | bytes 1179648 | tf_op jit(solution)/shard_map/all_to_all | solution.py:239
  355.9 1.4 copy.472
  357.3 14.3 %all-to-all-done.2 = f32[1,24,6,8,128]{4,1,2,0,3:T(8,128)S(1)} async-done(((f32[1,24,6,8,128]{4,1,2,0,3:T(8,128)}), f32[1,24,6,8,128]{4,1,2,0,3:T(8,128)S(1)}, u32[]{:S(2)}, u32[]{:S(2)}) %all-to-all-start.2) | async-done | bytes 589856 | tf_op jit(solution)/shard_map/all_to_all | solution.py:239
  371.6 1.4 copy.473
  (749 shorter events, 34.9 us)
Async XLA Ops:
  7.7 1.0 copy-start.13
  7.8 219.3 %copy-start.254 = (f32[32]{0:T(128)S(1)}, f32[32]{0:T(128)}, u32[]{:S(2)}) copy-start(f32[32]{0:T(128)} %param.7) | copy-start | bytes 388
  228.6 57.7 %all-to-all-start = ((f32[8,24,6,1,128]{4,1,3,2,0:T(8,128)}), f32[8,24,6,1,128]{4,1,3,2,0:T(8,128)S(1)}, u32[]{:S(2)}, u32[]{:S(2)}) async-start(f32[8,24,6,1,128]{4,1,3,2,0:T(8,128)} %copy.465), calls=%async_computation | async-start | bytes 1179648 | tf_op jit(solution)/shard_map/all_to_all | solution.py:185
  264.2 20.5 %collective-permute-start.1 = (f32[18,1,8,128]{3,2,1,0:T(8,128)S(1)}, f32[18,1,8,128]{3,2,1,0:T(8,128)}, u32[]{:S(2)}, u32[]{:S(2)}) collective-permute-start(f32[18,1,8,128]{3,2,1,0:T(8,128)S(1)} %slice_bitcast_fusion.1), channel_id=1, source_target_pairs={{0,1},{1,2},{2,3},{3,4},{4,5},{5,6},{6,7},{7,8},{8,9},{9,10},{10,1... | collective-permute-start | bytes 221192 | tf_op jit(solution)/shard_map/ppermute | solution.py:21
  273.4 2.5 copy-start
  277.4 2.4 copy-start.2
  279.0 1.6 copy-start.3
  279.8 30.5 %copy-start.170 = (f32[6,8,128]{2,1,0:T(8,128)}, f32[6,8,128]{2,1,0:T(8,128)S(1)}, u32[]{:S(2)}) copy-start(f32[6,8,128]{2,1,0:T(8,128)S(1)} %get-tuple-element.563) | copy-start | bytes 73732
  279.8 30.5 %copy-start.172 = (f32[6,8,128]{2,1,0:T(8,128)}, f32[6,8,128]{2,1,0:T(8,128)S(1)}, u32[]{:S(2)}) copy-start(f32[6,8,128]{2,1,0:T(8,128)S(1)} %get-tuple-element.570) | copy-start | bytes 73732
  279.8 30.5 %copy-start.174 = (f32[6,8,128]{2,1,0:T(8,128)}, f32[6,8,128]{2,1,0:T(8,128)S(1)}, u32[]{:S(2)}) copy-start(f32[6,8,128]{2,1,0:T(8,128)S(1)} %get-tuple-element.571) | copy-start | bytes 73732
  279.8 30.5 %copy-start.176 = (f32[6,8,128]{2,1,0:T(8,128)}, f32[6,8,128]{2,1,0:T(8,128)S(1)}, u32[]{:S(2)}) copy-start(f32[6,8,128]{2,1,0:T(8,128)S(1)} %get-tuple-element.613) | copy-start | bytes 73732
  279.8 30.5 %copy-start.178 = (f32[6,8,128]{2,1,0:T(8,128)}, f32[6,8,128]{2,1,0:T(8,128)S(1)}, u32[]{:S(2)}) copy-start(f32[6,8,128]{2,1,0:T(8,128)S(1)} %get-tuple-element.614) | copy-start | bytes 73732
  279.8 30.5 %copy-start.180 = (f32[6,8,128]{2,1,0:T(8,128)}, f32[6,8,128]{2,1,0:T(8,128)S(1)}, u32[]{:S(2)}) copy-start(f32[6,8,128]{2,1,0:T(8,128)S(1)} %get-tuple-element.621) | copy-start | bytes 73732
  279.8 3.0 copy-start.1
  283.6 34.6 %copy-start.26 = (f32[6,8,128]{2,1,0:T(8,128)}, f32[6,8,128]{2,1,0:T(8,128)S(1)}, u32[]{:S(2)}) copy-start(f32[6,8,128]{2,1,0:T(8,128)S(1)} %get-tuple-element.509) | copy-start | bytes 73732
  283.6 34.7 %copy-start.28 = (f32[6,8,128]{2,1,0:T(8,128)}, f32[6,8,128]{2,1,0:T(8,128)S(1)}, u32[]{:S(2)}) copy-start(f32[6,8,128]{2,1,0:T(8,128)S(1)} %get-tuple-element.516) | copy-start | bytes 73732
  283.6 34.7 %copy-start.30 = (f32[6,8,128]{2,1,0:T(8,128)}, f32[6,8,128]{2,1,0:T(8,128)S(1)}, u32[]{:S(2)}) copy-start(f32[6,8,128]{2,1,0:T(8,128)S(1)} %get-tuple-element.517) | copy-start | bytes 73732
  283.6 34.7 %copy-start.32 = (f32[6,8,128]{2,1,0:T(8,128)}, f32[6,8,128]{2,1,0:T(8,128)S(1)}, u32[]{:S(2)}) copy-start(f32[6,8,128]{2,1,0:T(8,128)S(1)} %get-tuple-element.650) | copy-start | bytes 73732
  283.6 34.7 %copy-start.34 = (f32[6,8,128]{2,1,0:T(8,128)}, f32[6,8,128]{2,1,0:T(8,128)S(1)}, u32[]{:S(2)}) copy-start(f32[6,8,128]{2,1,0:T(8,128)S(1)} %get-tuple-element.651) | copy-start | bytes 73732
  283.6 34.7 %copy-start.36 = (f32[6,8,128]{2,1,0:T(8,128)}, f32[6,8,128]{2,1,0:T(8,128)S(1)}, u32[]{:S(2)}) copy-start(f32[6,8,128]{2,1,0:T(8,128)S(1)} %get-tuple-element.658) | copy-start | bytes 73732
  286.2 33.2 %copy-start.14 = (f32[6,8,128]{2,1,0:T(8,128)}, f32[6,8,128]{2,1,0:T(8,128)S(1)}, u32[]{:S(2)}) copy-start(f32[6,8,128]{2,1,0:T(8,128)S(1)} %get-tuple-element.491) | copy-start | bytes 73732
  286.2 33.2 %copy-start.16 = (f32[6,8,128]{2,1,0:T(8,128)}, f32[6,8,128]{2,1,0:T(8,128)S(1)}, u32[]{:S(2)}) copy-start(f32[6,8,128]{2,1,0:T(8,128)S(1)} %get-tuple-element.498) | copy-start | bytes 73732
  286.2 33.3 %copy-start.18 = (f32[6,8,128]{2,1,0:T(8,128)}, f32[6,8,128]{2,1,0:T(8,128)S(1)}, u32[]{:S(2)}) copy-start(f32[6,8,128]{2,1,0:T(8,128)S(1)} %get-tuple-element.499) | copy-start | bytes 73732
  286.2 33.3 %copy-start.20 = (f32[6,8,128]{2,1,0:T(8,128)}, f32[6,8,128]{2,1,0:T(8,128)S(1)}, u32[]{:S(2)}) copy-start(f32[6,8,128]{2,1,0:T(8,128)S(1)} %get-tuple-element.659) | copy-start | bytes 73732
  286.3 33.3 %copy-start.22 = (f32[6,8,128]{2,1,0:T(8,128)}, f32[6,8,128]{2,1,0:T(8,128)S(1)}, u32[]{:S(2)}) copy-start(f32[6,8,128]{2,1,0:T(8,128)S(1)} %get-tuple-element.660) | copy-start | bytes 73732
  286.3 33.3 %copy-start.24 = (f32[6,8,128]{2,1,0:T(8,128)}, f32[6,8,128]{2,1,0:T(8,128)S(1)}, u32[]{:S(2)}) copy-start(f32[6,8,128]{2,1,0:T(8,128)S(1)} %get-tuple-element.667) | copy-start | bytes 73732
  286.3 33.9 %all-to-all-start.1 = ((f32[8,24,6,1,128]{4,1,3,2,0:T(8,128)}), f32[8,24,6,1,128]{4,1,3,2,0:T(8,128)S(1)}, u32[]{:S(2)}, u32[]{:S(2)}) async-start(f32[8,24,6,1,128]{4,1,3,2,0:T(8,128)} %copy.467), calls=%async_computation.1 | async-start | bytes 1179648 | tf_op jit(solution)/shard_map/all_to_all | solution.py:184
  293.6 23.4 %collective-permute-start.2 = (f32[1,24,1,8,128]{4,3,2,1,0:T(8,128)S(1)}, f32[1,24,1,8,128]{4,3,2,1,0:T(8,128)S(1)}, u32[]{:S(2)}, u32[]{:S(2)}) collective-permute-start(f32[1,24,1,8,128]{4,3,2,1,0:T(8,128)S(1)} %get-tuple-element.256), channel_id=1, source_target_pairs={{0,1},{1,2},{2,3},{3,4},{4,5},{5,6},{6,7},{7,8},{8,9},{9,10},{10,1... | collective-permute-start | bytes 294920 | tf_op jit(solution)/shard_map/ppermute | solution.py:31
  297.6 19.4 %collective-permute-start = (f32[1,24,1,8,128]{4,3,2,1,0:T(8,128)S(1)}, f32[1,24,1,8,128]{4,3,2,1,0:T(8,128)S(1)}, u32[]{:S(2)}, u32[]{:S(2)}) collective-permute-start(f32[1,24,1,8,128]{4,3,2,1,0:T(8,128)S(1)} %get-tuple-element.257), channel_id=1, source_target_pairs={{1,0},{2,1},{3,2},{4,3},{5,4},{6,5},{7,6},{8,7},{9,8},{10,9},{11,1... | collective-permute-start | bytes 294920 | tf_op jit(solution)/shard_map/ppermute | solution.py:32
  329.8 15.0 %collective-permute-start.4 = (f32[1,24,1,8,128]{4,3,2,1,0:T(8,128)S(1)}, f32[1,24,1,8,128]{4,3,2,1,0:T(8,128)S(1)}, u32[]{:S(2)}, u32[]{:S(2)}) collective-permute-start(f32[1,24,1,8,128]{4,3,2,1,0:T(8,128)S(1)} %get-tuple-element.242), channel_id=1, source_target_pairs={{0,1},{1,2},{2,3},{3,4},{4,5},{5,6},{6,7},{7,8},{8,9},{9,10},{10,1... | collective-permute-start | bytes 294920 | tf_op jit(solution)/shard_map/ppermute | solution.py:31
  331.7 13.1 %collective-permute-start.3 = (f32[1,24,1,8,128]{4,3,2,1,0:T(8,128)S(1)}, f32[1,24,1,8,128]{4,3,2,1,0:T(8,128)S(1)}, u32[]{:S(2)}, u32[]{:S(2)}) collective-permute-start(f32[1,24,1,8,128]{4,3,2,1,0:T(8,128)S(1)} %get-tuple-element.243), channel_id=1, source_target_pairs={{1,0},{2,1},{3,2},{4,3},{5,4},{6,5},{7,6},{8,7},{9,8},{10,9},{11,1... | collective-permute-start | bytes 294920 | tf_op jit(solution)/shard_map/ppermute | solution.py:32
  349.4 22.3 %all-to-all-start.2 = ((f32[1,24,6,8,128]{4,1,2,0,3:T(8,128)}), f32[1,24,6,8,128]{4,1,2,0,3:T(8,128)S(1)}, u32[]{:S(2)}, u32[]{:S(2)}) async-start(f32[1,24,6,8,128]{4,1,2,0,3:T(8,128)} %copy.470), calls=%async_computation.2 | async-start | bytes 1179648 | tf_op jit(solution)/shard_map/all_to_all | solution.py:239
  (231 other events, 183.7 us)
